TPU v7x, 128 devices: a whole 4x4x4 slice. The times are simulated.
128 devices in a mesh: row: 16 (over z, x), vec: 8 (over y, core).
Axes of the slice: x: 4, y: 4, z: 4, core: 2. Of those that a mesh axis runs over, the one named last changes fastest.
Arguments:
- vectors: float32 [32768, 1024], P('row', 'vec'), may hold values from -8 to 8
- hamiltonian: float32 [256, 12, 128, 128], P('row'), may hold values from -0.15 to 0.15, as said below
- column_blocks: int32 [256, 12], P('row'), may hold values from 0 to 255, as said below
- live_counts: int32 [256], P('row'), may hold values from 3 to 12
- lower_bound: float32 [1], replicated, may hold values from -0.85 to -0.65
- upper_bound: float32 [1], replicated, may hold values from 1.05 to 1.3
Outputs:
- filtered: float32 [32768, 1024], P('row', 'vec')
Inputs may be any that keep to these rules, and one draw needn't show every extreme that they name: column_blocks[i, 0] = i, and every entry lies within 16 block rows of its row i, cyclically modulo 256; the distances 16 and -16 both occur. `hamiltonian`: H is symmetric: for every used slot of block row i that names column block j there is a used slot of block row j that names i and holds the transpose of its block, and slot 0 of every block row holds a symmetric block.
All inputs are finite; a program needn't handle non-finite values.
Results may differ from a plain program's by a relative error of at most 0.0003.
Values sent between devices are 32-bit elements; how exact they have to be, the bound alone decides.
No kernel may reach another device: no remote copies, remote signals or barrier semaphores. Data moves between devices by JAX's collectives and lax.ppermute only.
A program may use at most 128 MiB of HBM per device.

v0:
```python
import math
import jax
import jax.numpy as jnp
from jax import lax
from jax.sharding import PartitionSpec as P

NV = 1024
NS_ITERS = 3


def with_halo(cells, sides, width):
    for axis, dim in sides:
        count = lax.axis_size(axis)
        head = lax.slice_in_dim(cells, 0, width, axis=dim)
        tail = lax.slice_in_dim(cells, cells.shape[dim] - width, cells.shape[dim], axis=dim)
        cells = jnp.concatenate(
            [
                lax.ppermute(tail, axis, [(i, (i + 1) % count) for i in range(count)]),
                cells,
                lax.ppermute(head, axis, [((i + 1) % count, i) for i in range(count)]),
            ],
            axis=dim,
        )
    return cells


def on_device(vectors, hamiltonian, column_blocks, live_counts, lower_bound, upper_bound):
    rows_dev, panel_cols = vectors.shape
    block_rows, slot_count, block_size, unused_size = hamiltonian.shape
    row_count = lax.axis_size("row")
    first_row = lax.axis_index("row") * block_rows
    local_cols = (column_blocks - first_row + block_rows) % (block_rows * row_count)

    def apply_field(operand):
        widened = with_halo(operand, (("row", 0),), block_rows * block_size)
        widened_blocks = widened.reshape(3 * block_rows, block_size, panel_cols)
        picked = jnp.take(widened_blocks, local_cols, axis=0)
        live_mask = (
            jnp.arange(slot_count, dtype=jnp.int32)[None, :] < live_counts[:, None]
        ).astype(jnp.float32)
        summed = jnp.einsum(
            "rkij,rkjc->ric",
            hamiltonian,
            picked * live_mask[:, :, None, None],
            precision=lax.Precision.HIGHEST,
            preferred_element_type=jnp.float32,
        )
        return summed.reshape(rows_dev, panel_cols)

    centre = (upper_bound[0] + lower_bound[0]) / 2
    radius = (upper_bound[0] - lower_bound[0]) / 2
    first = (apply_field(vectors) - centre * vectors) / radius
    second = 2 * (apply_field(first) - centre * first) / radius - vectors
    energy = lax.psum(jnp.sum(second * second), ("row", "vec"))
    current = second * jnp.sqrt(NV / (4 * (energy + 1e-06)))
    stacked = current
    for iteration in range(NS_ITERS):
        stacked = lax.all_to_all(current, "vec", split_axis=0, concat_axis=1, tiled=True)
        local_gram = jnp.einsum(
            "rc,rd->cd",
            stacked,
            stacked,
            precision=lax.Precision.HIGHEST,
            preferred_element_type=jnp.float32,
        )
        gram = lax.psum(local_gram, ("row", "vec"))
        stacked = 1.5 * stacked - 0.5 * jnp.dot(
            stacked, gram, precision=lax.Precision.HIGHEST, preferred_element_type=jnp.float32
        )
        current = lax.all_to_all(stacked, "vec", split_axis=1, concat_axis=0, tiled=True)
    total_rows = rows_dev * row_count
    return current * math.sqrt(total_rows)


def solution(mesh):
    placed = (P("row", "vec"), P("row", None, None, None), P("row", None), P("row"), P(), P())
    return jax.shard_map(
        on_device, mesh=mesh, in_specs=placed, out_specs=P("row", "vec"), check_vma=False
    )
```

profile of v0, /device:TPU:1, one launch (start us, length us, event | category | flops | bytes accessed | tf_op | source)
XLA Modules:
  0.0 796.7 jit_solution(12494661973624520224)
XLA Ops:
  6.5 6.8 collective-permute-start.1
  15.5 20.0 %collective-permute-done.1 = f32[2048,128]{1,0:T(8,128)S(1)} collective-permute-done((f32[2048,128]{1,0:T(8,128)}, f32[2048,128]{1,0:T(8,128)S(1)}, u32[]{:S(2)}, u32[]{:S(2)}) %collective-permute-start.1) | collective-permute-done | bytes 1048608 | tf_op jit(solution)/shard_map/ppermute | solution.py:20
  42.8 5.9 gather_fusion
  48.7 19.3 %fusion.1 = f32[16,128,128,1]{1,2,3,0:T(8,128)S(1)} fusion(f32[16,12,128,128]{3,2,1,0:T(8,128)} %param.9, f32[16,12,128,128]{3,2,1,0:T(8,128)} %bitcast.112, f32[16,12]{1,0:T(8,128)S(1)} %get-tuple-element.10, pred[16,12]{1,0:T(8,128)(4,1)S(1)} %get-tuple-element.8), kind=kOutput, calls=%fused_computation.5 | convolution fusion | flops 4838129664 | bytes 26215360 | tf_op jit(solution)/shard_map/rkij,rkjc->ric/dot_general | solution.py:41
  69.7 21.4 %collective-permute-done.3 = f32[2048,128]{1,0:T(8,128)S(1)} collective-permute-done((f32[2048,128]{1,0:T(8,128)S(1)}, f32[2048,128]{1,0:T(8,128)S(1)}, u32[]{:S(2)}, u32[]{:S(2)}) %collective-permute-start.3) | collective-permute-done | bytes 1048608 | tf_op jit(solution)/shard_map/ppermute | solution.py:20
  91.1 4.5 collective-permute-done.2
  95.8 5.9 gather_fusion.1
  101.7 19.4 %fusion = f32[16,128,128,1]{1,2,3,0:T(8,128)S(1)} fusion(f32[16,12,128,128]{3,2,1,0:T(8,128)} %param.9, f32[16,12,128,128]{3,2,1,0:T(8,128)} %bitcast.111, f32[16,12]{1,0:T(8,128)S(1)} %get-tuple-element.10, pred[16,12]{1,0:T(8,128)(4,1)S(1)} %get-tuple-element.8), kind=kOutput, calls=%fused_computation.3 | convolution fusion | flops 4838129664 | bytes 26215360 | tf_op jit(solution)/shard_map/rkij,rkjc->ric/dot_general | solution.py:41
  122.1 65.0 %psum.28 = f32[]{:T(128)} all-reduce(f32[]{:T(128)} %get-tuple-element.6), channel_id=1, replica_groups=mesh['row'=16,'vec'=8] {'row','vec'}, use_global_device_ids=true, to_apply=%region_1.3 | all-reduce | flops 1 | bytes 8 | tf_op jit(solution)/shard_map/psum | solution.py:54
  187.9 19.4 %all_to_all.96 = f32[8,256,128]{2,1,0:T(8,128)S(1)} all-to-all(f32[8,256,128]{2,1,0:T(8,128)S(1)} %bitcast.113), channel_id=1, replica_groups=mesh['row'=16,'vec'=8] {'vec'}, dimensions={0} | all-to-all | bytes 2097152 | tf_op jit(solution)/shard_map/all_to_all | solution.py:58
  207.2 5.1 fusion.21
  212.4 150.4 %all-reduce.4.cloned.1.call-done = f32[1024,1024]{1,0:T(8,128)} async-done(((f32[1024,1024]{1,0:T(8,128)}), f32[1024,1024]{1,0:T(8,128)}) %all-reduce.4.cloned.1.call-update) | async-done | bytes 4194320 | tf_op jit(solution)/shard_map/psum | solution.py:66
  362.8 5.8 fusion.13
  368.7 19.7 %all_to_all.97 = f32[256,8,128]{2,0,1:T(8,128)S(1)} all-to-all(f32[256,8,128]{2,0,1:T(8,128)S(1)} %bitcast.114), channel_id=1, replica_groups=mesh['row'=16,'vec'=8] {'vec'}, dimensions={1} | all-to-all | bytes 2097152 | tf_op jit(solution)/shard_map/all_to_all | solution.py:70
  388.4 18.4 %all_to_all.98 = f32[8,256,128]{2,1,0:T(8,128)S(1)} all-to-all(f32[8,256,128]{2,1,0:T(8,128)S(1)} %bitcast.115), channel_id=1, replica_groups=mesh['row'=16,'vec'=8] {'vec'}, dimensions={0} | all-to-all | bytes 2097152 | tf_op jit(solution)/shard_map/all_to_all | solution.py:58
  406.8 5.1 fusion.18
  411.9 151.2 %all-reduce.6.cloned.1.call-done = f32[1024,1024]{1,0:T(8,128)} async-done(((f32[1024,1024]{1,0:T(8,128)}), f32[1024,1024]{1,0:T(8,128)}) %all-reduce.6.cloned.1.call-update) | async-done | bytes 4194320 | tf_op jit(solution)/shard_map/psum | solution.py:66
  563.1 5.8 fusion.11
  569.0 19.7 %all_to_all.99 = f32[256,8,128]{2,0,1:T(8,128)S(1)} all-to-all(f32[256,8,128]{2,0,1:T(8,128)S(1)} %bitcast.116), channel_id=1, replica_groups=mesh['row'=16,'vec'=8] {'vec'}, dimensions={1} | all-to-all | bytes 2097152 | tf_op jit(solution)/shard_map/all_to_all | solution.py:70
  588.7 18.4 %all_to_all.100 = f32[8,256,128]{2,1,0:T(8,128)S(1)} all-to-all(f32[8,256,128]{2,1,0:T(8,128)S(1)} %bitcast.117), channel_id=1, replica_groups=mesh['row'=16,'vec'=8] {'vec'}, dimensions={0} | all-to-all | bytes 2097152 | tf_op jit(solution)/shard_map/all_to_all | solution.py:58
  607.1 5.1 fusion.15
  612.2 151.4 %all-reduce.8.cloned.1.call-done = f32[1024,1024]{1,0:T(8,128)} async-done(((f32[1024,1024]{1,0:T(8,128)}), f32[1024,1024]{1,0:T(8,128)}) %all-reduce.8.cloned.1.call-update) | async-done | bytes 4194320 | tf_op jit(solution)/shard_map/psum | solution.py:66
  763.5 5.8 fusion.9
  769.4 19.7 %all_to_all.101 = f32[256,8,128]{2,0,1:T(8,128)S(1)} all-to-all(f32[256,8,128]{2,0,1:T(8,128)S(1)} %bitcast.118), channel_id=1, replica_groups=mesh['row'=16,'vec'=8] {'vec'}, dimensions={1} | all-to-all | bytes 2097152 | tf_op jit(solution)/shard_map/all_to_all | solution.py:70
  (32 shorter events, 12.5 us)
Async XLA Ops:
  6.5 356.3 %all-reduce.4.cloned.1.call-start = ((), (), s32[]{:S(2)}) async-start(), calls=%async_computation.6 | async-start | bytes 8388608 | tf_op jit(solution)/shard_map/psum | solution.py:66
  6.5 28.9 %collective-permute-start.1 = (f32[2048,128]{1,0:T(8,128)}, f32[2048,128]{1,0:T(8,128)S(1)}, u32[]{:S(2)}, u32[]{:S(2)}) collective-permute-start(f32[2048,128]{1,0:T(8,128)} %param.8), channel_id=1, source_target_pairs={{8,0},{16,8},{24,16},{32,24},{40,32},{48,40},{56,48},{64,56},{72,6... | collective-permute-start | bytes 3145736 | tf_op jit(solution)/shard_map/ppermute | solution.py:20
  13.3 27.4 %collective-permute-start = (f32[2048,128]{1,0:T(8,128)}, f32[2048,128]{1,0:T(8,128)}, u32[]{:S(2)}, u32[]{:S(2)}) collective-permute-start(f32[2048,128]{1,0:T(8,128)} %param.8), channel_id=1, source_target_pairs={{0,8},{8,16},{16,24},{24,32},{32,40},{40,48},{48,56},{56,64},{64,7... | collective-permute-start | bytes 3145736 | tf_op jit(solution)/shard_map/ppermute | solution.py:18
  35.5 1.0 copy-start.4
  48.7 19.3 %copy-start.2 = (f32[2048,128]{1,0:T(8,128)S(1)}, f32[2048,128]{1,0:T(8,128)}, u32[]{:S(2)}) copy-start(f32[2048,128]{1,0:T(8,128)} %param.8) | copy-start | bytes 3145732
  68.0 27.8 %copy-start = (f32[16,128,128,1]{1,2,3,0:T(8,128)}, f32[16,128,128,1]{1,2,3,0:T(8,128)S(1)}, u32[]{:S(2)}) copy-start(f32[16,128,128,1]{1,2,3,0:T(8,128)S(1)} %fusion.1) | copy-start | bytes 3145732
  68.1 23.0 %collective-permute-start.3 = (f32[2048,128]{1,0:T(8,128)S(1)}, f32[2048,128]{1,0:T(8,128)S(1)}, u32[]{:S(2)}, u32[]{:S(2)}) collective-permute-start(f32[2048,128]{1,0:T(8,128)S(1)} %fusion.26), channel_id=1, source_target_pairs={{8,0},{16,8},{24,16},{32,24},{40,32},{48,40},{56,48},{64,56},{72,6... | collective-permute-start | bytes 3145736 | tf_op jit(solution)/shard_map/ppermute | solution.py:20
  69.4 26.2 %collective-permute-start.2 = (f32[2048,128]{1,0:T(8,128)S(1)}, f32[2048,128]{1,0:T(8,128)S(1)}, u32[]{:S(2)}, u32[]{:S(2)}) collective-permute-start(f32[2048,128]{1,0:T(8,128)S(1)} %fusion.26), channel_id=1, source_target_pairs={{0,8},{8,16},{16,24},{24,32},{32,40},{40,48},{48,56},{56,64},{64,7... | collective-permute-start | bytes 3145736 | tf_op jit(solution)/shard_map/ppermute | solution.py:18
  101.7 19.4 %copy-start.1 = (f32[16,128,128,1]{1,2,3,0:T(8,128)S(1)}, f32[16,128,128,1]{1,2,3,0:T(8,128)}, u32[]{:S(2)}) copy-start(f32[16,128,128,1]{1,2,3,0:T(8,128)} %copy-done) | copy-start | bytes 3145732
  101.7 19.4 %copy-start.3 = (f32[2048,128]{1,0:T(8,128)S(1)}, f32[2048,128]{1,0:T(8,128)}, u32[]{:S(2)}) copy-start(f32[2048,128]{1,0:T(8,128)} %param.8) | copy-start | bytes 3145732
  212.3 350.8 %all-reduce.6.cloned.1.call-start = ((), (), s32[]{:S(2)}) async-start(), calls=%async_computation.7 | async-start | bytes 8388608 | tf_op jit(solution)/shard_map/psum | solution.py:66
  411.9 351.7 %all-reduce.8.cloned.1.call-start = ((), (), s32[]{:S(2)}) async-start(), calls=%async_computation.8 | async-start | bytes 8388608 | tf_op jit(solution)/shard_map/psum | solution.py:66
Sparse Core Ops, SparseCore 0:
  212.5 150.3 all-reduce.3
  412.0 151.0 all-reduce.5
  612.3 151.1 all-reduce.7
where the time goes:
time: 797 us
  waiting for transfers between devices  503 us (63%)
  blocking collectives  180 us (23%)
  matrix products  71.3 us (9%)
  between operations  15.3 us (2%)
  local copies, waits for them, and re-layouts  13.1 us (2%)
  starting transfers between devices  8.39 us (1%)
    psum x3, waiting for transfers between devices, on_device(): gram = lax.psum(local_gram, ('row', 'vec'))  453 us
    psum x1, blocking collectives, on_device(): energy = lax.psum(jnp.sum(second * second), ('row', 'vec'))  65 us
    all_to_all x3, blocking collectives, on_device(): lax.all_to_all(stacked, 'vec', split_axis=1, concat_axis=0, tiled=True)  59.1 us
    all_to_all x3, blocking collectives, on_device(): lax.all_to_all(current, 'vec', split_axis=0, concat_axis=1, tiled=True)  56.1 us
    ppermute x2, waiting for transfers between devices, with_halo(): lax.ppermute(head, axis, [((i + 1) % count, i) for i in range(count)])  41.4 us
    dot_general x2, matrix products, apply_field(): jnp.einsum('rkij,rkjc->ric', hamiltonian, picked * live_mask[:, :, None,...  38.7 us
    dot_general x3, matrix products, on_device(): jnp.dot(stacked, gram, precision=lax.Precision.HIGHEST, preferred_element...  17.4 us
  transfers between devices with their start and end apart: 7, of which 7 were waited for; matrix products, arithmetic and copies ran while one was open for 0% of the time, Pallas kernels for 0%

commit v1 on v0

--- a/solution.py
+++ b/solution.py
@@ -63,7 +63,7 @@
             precision=lax.Precision.HIGHEST,
             preferred_element_type=jnp.float32,
         )
-        gram = lax.psum(local_gram, ("row", "vec"))
+        gram = lax.psum(lax.psum(local_gram, "row"), "vec")
         stacked = 1.5 * stacked - 0.5 * jnp.dot(
             stacked, gram, precision=lax.Precision.HIGHEST, preferred_element_type=jnp.float32
         )

time: 797 us -> 871 us (1.093)
  waiting for transfers between devices: 503 us -> 575 us
    psum x3 -> x6, waiting for transfers between devices: 453 us -> 525 us  [on_device(): gram = lax.psum(lax.psum(local_gram, 'row'), 'vec')]
  transfers between devices with their start and end apart: 7 -> 10, of which waited for: 7 -> 10; matrix products, arithmetic and copies ran while one was open for 0% -> 0% of each run, Pallas kernels for 0% -> 0%
where the time goes in v1:
time: 871 us
  waiting for transfers between devices  575 us (66%)
  blocking collectives  182 us (21%)
  matrix products  71.3 us (8%)
  between operations  15.7 us (2%)
  local copies, waits for them, and re-layouts  13.1 us (2%)
  starting transfers between devices  8.77 us (1%)
    psum x6, waiting for transfers between devices, on_device(): gram = lax.psum(lax.psum(local_gram, 'row'), 'vec')  525 us
    psum x1, blocking collectives, on_device(): energy = lax.psum(jnp.sum(second * second), ('row', 'vec'))  65 us
    all_to_all x3, blocking collectives, on_device(): lax.all_to_all(stacked, 'vec', split_axis=1, concat_axis=0, tiled=True)  60.5 us
    all_to_all x3, blocking collectives, on_device(): lax.all_to_all(current, 'vec', split_axis=0, concat_axis=1, tiled=True)  56.1 us
    ppermute x2, waiting for transfers between devices, with_halo(): lax.ppermute(head, axis, [((i + 1) % count, i) for i in range(count)])  41.4 us
    dot_general x2, matrix products, apply_field(): jnp.einsum('rkij,rkjc->ric', hamiltonian, picked * live_mask[:, :, None,...  38.7 us
  transfers between devices with their start and end apart: 10, of which 10 were waited for; matrix products, arithmetic and copies ran while one was open for 0% of the time, Pallas kernels for 0%

profile of v1, /device:TPU:1, one launch (start us, length us, event | category | flops | bytes accessed | tf_op | source)
XLA Modules:
  0.0 870.8 jit_solution(159823368864319236)
XLA Ops:
  6.5 6.8 collective-permute-start.1
  15.5 20.0 %collective-permute-done.1 = f32[2048,128]{1,0:T(8,128)S(1)} collective-permute-done((f32[2048,128]{1,0:T(8,128)}, f32[2048,128]{1,0:T(8,128)S(1)}, u32[]{:S(2)}, u32[]{:S(2)}) %collective-permute-start.1) | collective-permute-done | bytes 1048608 | tf_op jit(solution)/shard_map/ppermute | solution.py:20
  42.8 5.9 gather_fusion
  48.7 19.3 %fusion.1 = f32[16,128,128,1]{1,2,3,0:T(8,128)S(1)} fusion(f32[16,12,128,128]{3,2,1,0:T(8,128)} %param.9, f32[16,12,128,128]{3,2,1,0:T(8,128)} %bitcast.112, f32[16,12]{1,0:T(8,128)S(1)} %get-tuple-element.10, pred[16,12]{1,0:T(8,128)(4,1)S(1)} %get-tuple-element.8), kind=kOutput, calls=%fused_computation.5 | convolution fusion | flops 4838129664 | bytes 26215360 | tf_op jit(solution)/shard_map/rkij,rkjc->ric/dot_general | solution.py:41
  69.7 21.4 %collective-permute-done.3 = f32[2048,128]{1,0:T(8,128)S(1)} collective-permute-done((f32[2048,128]{1,0:T(8,128)S(1)}, f32[2048,128]{1,0:T(8,128)S(1)}, u32[]{:S(2)}, u32[]{:S(2)}) %collective-permute-start.3) | collective-permute-done | bytes 1048608 | tf_op jit(solution)/shard_map/ppermute | solution.py:20
  95.8 5.9 gather_fusion.1
  101.7 19.4 %fusion = f32[16,128,128,1]{1,2,3,0:T(8,128)S(1)} fusion(f32[16,12,128,128]{3,2,1,0:T(8,128)} %param.9, f32[16,12,128,128]{3,2,1,0:T(8,128)} %bitcast.111, f32[16,12]{1,0:T(8,128)S(1)} %get-tuple-element.10, pred[16,12]{1,0:T(8,128)(4,1)S(1)} %get-tuple-element.8), kind=kOutput, calls=%fused_computation.3 | convolution fusion | flops 4838129664 | bytes 26215360 | tf_op jit(solution)/shard_map/rkij,rkjc->ric/dot_general | solution.py:41
  122.1 65.0 %psum.49 = f32[]{:T(128)} all-reduce(f32[]{:T(128)} %get-tuple-element.6), channel_id=1, replica_groups=mesh['row'=16,'vec'=8] {'row','vec'}, use_global_device_ids=true, to_apply=%region_1.3 | all-reduce | flops 1 | bytes 8 | tf_op jit(solution)/shard_map/psum | solution.py:54
  187.8 19.4 %all_to_all.96 = f32[8,256,128]{2,1,0:T(8,128)S(1)} all-to-all(f32[8,256,128]{2,1,0:T(8,128)S(1)} %bitcast.113), channel_id=1, replica_groups=mesh['row'=16,'vec'=8] {'vec'}, dimensions={0} | all-to-all | bytes 2097152 | tf_op jit(solution)/shard_map/all_to_all | solution.py:58
  207.2 5.1 fusion.21
  212.4 99.5 %all-reduce.7.cloned.1.call-done = f32[1024,1024]{1,0:T(8,128)} async-done(((f32[1024,1024]{1,0:T(8,128)}), f32[1024,1024]{1,0:T(8,128)}) %all-reduce.7.cloned.1.call-update) | async-done | bytes 4194320 | tf_op jit(solution)/shard_map/psum | solution.py:66
  312.0 73.1 %all-reduce.9.cloned.1.call-done = f32[1024,1024]{1,0:T(8,128)} async-done(((f32[1024,1024]{1,0:T(8,128)}), f32[1024,1024]{1,0:T(8,128)}) %all-reduce.9.cloned.1.call-update) | async-done | bytes 4194320 | tf_op jit(solution)/shard_map/psum | solution.py:66
  385.0 5.8 fusion.13
  390.9 20.2 %all_to_all.97 = f32[256,8,128]{2,0,1:T(8,128)S(1)} all-to-all(f32[256,8,128]{2,0,1:T(8,128)S(1)} %bitcast.114), channel_id=1, replica_groups=mesh['row'=16,'vec'=8] {'vec'}, dimensions={1} | all-to-all | bytes 2097152 | tf_op jit(solution)/shard_map/all_to_all | solution.py:70
  411.1 18.4 %all_to_all.98 = f32[8,256,128]{2,1,0:T(8,128)S(1)} all-to-all(f32[8,256,128]{2,1,0:T(8,128)S(1)} %bitcast.115), channel_id=1, replica_groups=mesh['row'=16,'vec'=8] {'vec'}, dimensions={0} | all-to-all | bytes 2097152 | tf_op jit(solution)/shard_map/all_to_all | solution.py:58
  434.6 103.3 %all-reduce.11.cloned.1.call-done = f32[1024,1024]{1,0:T(8,128)} async-done(((f32[1024,1024]{1,0:T(8,128)}), f32[1024,1024]{1,0:T(8,128)}) %all-reduce.11.cloned.1.call-update) | async-done | bytes 4194320 | tf_op jit(solution)/shard_map/psum | solution.py:66
  538.0 72.9 %all-reduce.13.cloned.1.call-done = f32[1024,1024]{1,0:T(8,128)} async-done(((f32[1024,1024]{1,0:T(8,128)}), f32[1024,1024]{1,0:T(8,128)}) %all-reduce.13.cloned.1.call-update) | async-done | bytes 4194320 | tf_op jit(solution)/shard_map/psum | solution.py:66
  610.9 5.8 fusion.11
  616.8 20.2 %all_to_all.99 = f32[256,8,128]{2,0,1:T(8,128)S(1)} all-to-all(f32[256,8,128]{2,0,1:T(8,128)S(1)} %bitcast.116), channel_id=1, replica_groups=mesh['row'=16,'vec'=8] {'vec'}, dimensions={1} | all-to-all | bytes 2097152 | tf_op jit(solution)/shard_map/all_to_all | solution.py:70
  637.0 18.4 %all_to_all.100 = f32[8,256,128]{2,1,0:T(8,128)S(1)} all-to-all(f32[8,256,128]{2,1,0:T(8,128)S(1)} %bitcast.117), channel_id=1, replica_groups=mesh['row'=16,'vec'=8] {'vec'}, dimensions={0} | all-to-all | bytes 2097152 | tf_op jit(solution)/shard_map/all_to_all | solution.py:58
  660.8 103.0 %all-reduce.15.cloned.1.call-done = f32[1024,1024]{1,0:T(8,128)} async-done(((f32[1024,1024]{1,0:T(8,128)}), f32[1024,1024]{1,0:T(8,128)}) %all-reduce.15.cloned.1.call-update) | async-done | bytes 4194320 | tf_op jit(solution)/shard_map/psum | solution.py:66
  763.8 73.0 %all-reduce.17.cloned.1.call-done = f32[1024,1024]{1,0:T(8,128)} async-done(((f32[1024,1024]{1,0:T(8,128)}), f32[1024,1024]{1,0:T(8,128)}) %all-reduce.17.cloned.1.call-update) | async-done | bytes 4194320 | tf_op jit(solution)/shard_map/psum | solution.py:66
  836.8 5.8 fusion.9
  842.7 20.2 %all_to_all.101 = f32[256,8,128]{2,0,1:T(8,128)S(1)} all-to-all(f32[256,8,128]{2,0,1:T(8,128)S(1)} %bitcast.118), channel_id=1, replica_groups=mesh['row'=16,'vec'=8] {'vec'}, dimensions={1} | all-to-all | bytes 2097152 | tf_op jit(solution)/shard_map/all_to_all | solution.py:70
  (41 shorter events, 27.5 us)
Async XLA Ops:
  6.5 305.4 %all-reduce.7.cloned.1.call-start = ((), (), s32[]{:S(2)}) async-start(), calls=%async_computation.6 | async-start | bytes 8388608 | tf_op jit(solution)/shard_map/psum | solution.py:66
  6.5 28.9 %collective-permute-start.1 = (f32[2048,128]{1,0:T(8,128)}, f32[2048,128]{1,0:T(8,128)S(1)}, u32[]{:S(2)}, u32[]{:S(2)}) collective-permute-start(f32[2048,128]{1,0:T(8,128)} %param.8), channel_id=1, source_target_pairs={{8,0},{16,8},{24,16},{32,24},{40,32},{48,40},{56,48},{64,56},{72,6... | collective-permute-start | bytes 3145736 | tf_op jit(solution)/shard_map/ppermute | solution.py:20
  13.3 27.4 %collective-permute-start = (f32[2048,128]{1,0:T(8,128)}, f32[2048,128]{1,0:T(8,128)}, u32[]{:S(2)}, u32[]{:S(2)}) collective-permute-start(f32[2048,128]{1,0:T(8,128)} %param.8), channel_id=1, source_target_pairs={{0,8},{8,16},{16,24},{24,32},{32,40},{40,48},{48,56},{56,64},{64,7... | collective-permute-start | bytes 3145736 | tf_op jit(solution)/shard_map/ppermute | solution.py:18
  35.5 1.0 copy-start.4
  48.7 19.3 %copy-start.2 = (f32[2048,128]{1,0:T(8,128)S(1)}, f32[2048,128]{1,0:T(8,128)}, u32[]{:S(2)}) copy-start(f32[2048,128]{1,0:T(8,128)} %param.8) | copy-start | bytes 3145732
  68.0 27.8 %copy-start = (f32[16,128,128,1]{1,2,3,0:T(8,128)}, f32[16,128,128,1]{1,2,3,0:T(8,128)S(1)}, u32[]{:S(2)}) copy-start(f32[16,128,128,1]{1,2,3,0:T(8,128)S(1)} %fusion.1) | copy-start | bytes 3145732
  68.1 23.0 %collective-permute-start.3 = (f32[2048,128]{1,0:T(8,128)S(1)}, f32[2048,128]{1,0:T(8,128)S(1)}, u32[]{:S(2)}, u32[]{:S(2)}) collective-permute-start(f32[2048,128]{1,0:T(8,128)S(1)} %fusion.26), channel_id=1, source_target_pairs={{8,0},{16,8},{24,16},{32,24},{40,32},{48,40},{56,48},{64,56},{72,6... | collective-permute-start | bytes 3145736 | tf_op jit(solution)/shard_map/ppermute | solution.py:20
  69.4 26.2 %collective-permute-start.2 = (f32[2048,128]{1,0:T(8,128)S(1)}, f32[2048,128]{1,0:T(8,128)S(1)}, u32[]{:S(2)}, u32[]{:S(2)}) collective-permute-start(f32[2048,128]{1,0:T(8,128)S(1)} %fusion.26), channel_id=1, source_target_pairs={{0,8},{8,16},{16,24},{24,32},{32,40},{40,48},{48,56},{56,64},{64,7... | collective-permute-start | bytes 3145736 | tf_op jit(solution)/shard_map/ppermute | solution.py:18
  101.7 19.4 %copy-start.1 = (f32[16,128,128,1]{1,2,3,0:T(8,128)S(1)}, f32[16,128,128,1]{1,2,3,0:T(8,128)}, u32[]{:S(2)}) copy-start(f32[16,128,128,1]{1,2,3,0:T(8,128)} %copy-done) | copy-start | bytes 3145732
  101.7 19.4 %copy-start.3 = (f32[2048,128]{1,0:T(8,128)S(1)}, f32[2048,128]{1,0:T(8,128)}, u32[]{:S(2)}) copy-start(f32[2048,128]{1,0:T(8,128)} %param.8) | copy-start | bytes 3145732
  212.3 172.7 %all-reduce.9.cloned.1.call-start = ((), (), s32[]{:S(2)}) async-start(), calls=%async_computation.7 | async-start | bytes 8388608 | tf_op jit(solution)/shard_map/psum | solution.py:66
  311.9 226.0 %all-reduce.11.cloned.1.call-start = ((), (), s32[]{:S(2)}) async-start(), calls=%async_computation.8 | async-start | bytes 8388608 | tf_op jit(solution)/shard_map/psum | solution.py:66
  434.6 176.3 %all-reduce.13.cloned.1.call-start = ((), (), s32[]{:S(2)}) async-start(), calls=%async_computation.9 | async-start | bytes 8388608 | tf_op jit(solution)/shard_map/psum | solution.py:66
  537.9 225.9 %all-reduce.15.cloned.1.call-start = ((), (), s32[]{:S(2)}) async-start(), calls=%async_computation.10 | async-start | bytes 8388608 | tf_op jit(solution)/shard_map/psum | solution.py:66
  660.4 176.3 %all-reduce.17.cloned.1.call-start = ((), (), s32[]{:S(2)}) async-start(), calls=%async_computation.11 | async-start | bytes 8388608 | tf_op jit(solution)/shard_map/psum | solution.py:66
Sparse Core Ops, SparseCore 0:
  212.4 99.3 all-reduce.6
  314.3 70.7 all-reduce.8
  434.7 103.1 all-reduce.10
  540.1 70.7 all-reduce.12
  660.6 103.1 all-reduce.14
  766.0 70.7 all-reduce.16
